TPU v7x, 32 devices: a whole 2x2x4 slice. The times are simulated.
32 devices in a mesh: energy: 8 (over z, x), slab: 2 (over core), rep: 2 (over y).
Axes of the slice: x: 2, y: 2, z: 4, core: 2. Of those that a mesh axis runs over, the one named last changes fastest.
Arguments:
- green_blocks: bfloat16 [8, 2, 512, 512], P('energy', 'slab', 'rep'), may hold values from -1 to 1
- occupation: float32 [8], P('energy'), may hold values from 0.1 to 1
- offsets: int32 [2], replicated, may hold values from 1 to 4, as said below
- coulomb: float32 [2, 512, 512], P('slab', 'rep'), may hold values from -0.9 to 0.9
- hamiltonian: float32 [2, 512, 512], P('slab', 'rep'), may hold values from -0.25 to 0.25
- onsite_level: float32 [8], P('energy'), may hold values from 2 to 3
- green_steps: int32 [8], P('energy'), may hold values from 1 to 2, as said below
- screen_steps: int32 [2], replicated, may hold values from 0 to 2, as said below
Outputs:
- green_next: float32 [8, 2, 512, 512], P('energy', 'slab', 'rep')
- screened: bfloat16 [2, 2, 512, 512], P(None, 'slab', 'rep')
Inputs may be any that keep to these rules, and one draw needn't show every extreme that they name: `offsets`: some frequency has offset 4; every other frequency has a smaller one. `green_steps`: some energy takes 2 turns. `screen_steps`: some frequency takes 2 turns; every other frequency takes fewer.
All inputs are finite; a program needn't handle non-finite values.
Results may differ from a plain program's by a relative error of at most 0.0004.
Values may be sent and summed in bfloat16 or wider, within the bound.
No kernel may reach another device: no remote copies, remote signals or barrier semaphores. Data moves between devices by JAX's collectives and lax.ppermute only.
A program may use at most 64 MiB of HBM per device.

v0:
```python
import jax
import jax.numpy as jnp
from jax import lax
from jax.sharding import PartitionSpec as P

SHIFTS = 4
FREQS = 2
NG = 2
NW = 2
precise = lax.Precision.HIGHEST


def from_behind(block, axis, distance):
    devices = range(lax.axis_size(axis))
    route = [(i - distance, i) for i in devices if i - distance in devices]
    return lax.ppermute(block, axis, route)


def broadcast(block, axis, owner):
    block = jnp.where(lax.axis_index(axis) == owner, block, jnp.zeros_like(block))
    return lax.psum(block, axis)


def with_halo(value, sides, width):
    for axis, dim in sides:
        peers, length = (lax.axis_size(axis), value.shape[dim])
        up = [(i, (i + 1) % peers) for i in range(peers - 1)]
        down = [(j, i) for i, j in up]
        last = lax.slice_in_dim(value, length - width, length, axis=dim)
        first = lax.slice_in_dim(value, 0, width, axis=dim)
        before = lax.ppermute(last, axis, up)
        after = lax.ppermute(first, axis, down)
        value = jnp.concatenate([before, value, after], axis=dim)
    return value


def row_product(first_factor, second_factor):
    return jnp.einsum("esij,esjk->esik", first_factor, second_factor, precision=precise)


def full_rows(block_rows):
    return lax.all_gather(block_rows, "rep", axis=2, tiled=True)


def newton_rows(operator, initial, known_full, counts, turn_total):
    operator_full = lax.all_gather(operator, "rep", axis=2, tiled=True)
    iterate = initial
    for turn_index in range(turn_total):
        if turn_index == 0 and known_full is not None:
            iterate_full = known_full
        else:
            iterate_full = full_rows(iterate)
        composed = row_product(row_product(iterate, operator_full), iterate_full)
        iterate = jnp.where(
            (turn_index < counts)[:, None, None, None], 2.0 * iterate - composed, iterate
        )
    return iterate


def body(
    green_blocks, occupation, offsets, coulomb, hamiltonian, onsite_level, green_steps, screen_steps
):
    local_count, _, half_rows, full_width = green_blocks.shape
    energies = local_count * lax.axis_size("energy")
    entry_scale = full_width ** (-0.5)
    shift_count = -(-SHIFTS // local_count)
    pieces = []
    received = green_blocks
    for distance in range(1, shift_count + 1):
        received = from_behind(received, "energy", 1)
        pieces.insert(0, received)
    extended = jnp.concatenate(pieces + [green_blocks], axis=0)
    anchor = shift_count * local_count
    lowered = jnp.stack(
        [
            lax.dynamic_slice_in_dim(extended, anchor - offsets[index], local_count, 0)
            for index in range(FREQS)
        ]
    )
    lowered_wide = lowered.astype(jnp.float32)
    weighted = occupation[:, None, None, None] * green_blocks.astype(jnp.float32)
    partial_value = jnp.sum(weighted[None] * lowered_wide, axis=1) * energies ** (-0.5)
    polarization = lax.psum(partial_value, "energy")
    rep_start = lax.axis_index("rep") * half_rows
    col_index = lax.broadcasted_iota(jnp.int32, (half_rows, full_width), 1)
    row_index = lax.broadcasted_iota(jnp.int32, (half_rows, full_width), 0) + rep_start
    identity_rows = (col_index == row_index).astype(jnp.float32)
    identity_full = jnp.eye(full_width, dtype=jnp.float32)[None, None]
    owner_index = lax.axis_index("energy") % FREQS
    polar_own = lax.dynamic_index_in_dim(polarization, owner_index, 0, keepdims=True)
    screen_operator = identity_rows + entry_scale * coulomb[None] * polar_own
    count_own = lax.dynamic_index_in_dim(screen_steps, owner_index, 0, keepdims=True)
    screen_start = jnp.broadcast_to(identity_rows, screen_operator.shape)
    inverse = newton_rows(screen_operator, screen_start, identity_full, count_own, NW)
    inverse_full = full_rows(inverse)
    screened_own = row_product(coulomb[None], inverse_full).astype(jnp.bfloat16)
    screened = jnp.stack([broadcast(screened_own, "energy", index)[0] for index in range(FREQS)])
    self_energy = (
        jnp.sum(lowered_wide * screened.astype(jnp.float32)[:, None], axis=0) * entry_scale
    )
    neighbours = with_halo(green_blocks, (("slab", 1),), 1)
    contact = (neighbours[:, 0:1].astype(jnp.float32) + neighbours[:, 2:3].astype(jnp.float32)) * (
        0.5 * entry_scale
    )
    dyson_rows = (
        onsite_level[:, None, None, None] * identity_rows
        + hamiltonian[None]
        - self_energy
        - contact
    )
    diagonal = jnp.sum(dyson_rows * identity_rows, axis=-1)
    initial = identity_rows * (1.0 / diagonal)[..., None]
    green_next = newton_rows(dyson_rows, initial, None, green_steps, NG)
    return (green_next, screened)


def solution(mesh):
    return jax.shard_map(
        body,
        mesh=mesh,
        in_specs=(
            P("energy", "slab", "rep", None),
            P("energy"),
            P(),
            P("slab", "rep", None),
            P("slab", "rep", None),
            P("energy"),
            P("energy"),
            P(),
        ),
        out_specs=(P("energy", "slab", "rep", None), P(None, "slab", "rep", None)),
        check_vma=False,
    )
```

profile of v0, /device:TPU:0, one launch (start us, length us, event | category | flops | bytes accessed | tf_op | source)
XLA Modules:
  0.0 359.1 jit_solution(1811731379270840315)
XLA Ops:
  8.3 4.9 %collective-permute-start = (bf16[1,1,256,512]{2,3,1,0:T(8,128)(2,1)S(1)}, bf16[1,1,256,512]{2,3,1,0:T(8,128)(2,1)S(1)}, u32[]{:S(2)}, u32[]{:S(2)}) collective-permute-start(bf16[1,1,256,512]{2,3,1,0:T(8,128)(2,1)S(1)} %copy.17), channel_id=1, source_target_pairs={{0,4},{4,8},{8,12},{12,16},{16,20},{20,24},{24,28},{1,5},{5,9},{9,... | collective-permute-start | bytes 786440 | tf_op jit(solution)/shard_map/ppermute | solution.py:16
  13.2 5.5 %collective-permute-done = bf16[1,1,256,512]{2,3,1,0:T(8,128)(2,1)S(1)} collective-permute-done((bf16[1,1,256,512]{2,3,1,0:T(8,128)(2,1)S(1)}, bf16[1,1,256,512]{2,3,1,0:T(8,128)(2,1)S(1)}, u32[]{:S(2)}, u32[]{:S(2)}) %collective-permute-start) | collective-permute-done | bytes 262176 | tf_op jit(solution)/shard_map/ppermute | solution.py:16
  18.7 4.4 %collective-permute-start.1 = (bf16[1,1,256,512]{2,3,1,0:T(8,128)(2,1)S(1)}, bf16[1,1,256,512]{2,3,1,0:T(8,128)(2,1)S(1)}, u32[]{:S(2)}, u32[]{:S(2)}) collective-permute-start(bf16[1,1,256,512]{2,3,1,0:T(8,128)(2,1)S(1)} %collective-permute-done), channel_id=1, source_target_pairs={{0,4},{4,8},{8,12},{12,16},{16,20},{20,24},{24,28},{1,5},{5,9},{9,... | collective-permute-start | bytes 786440 | tf_op jit(solution)/shard_map/ppermute | solution.py:16
  23.1 4.7 %collective-permute-done.1 = bf16[1,1,256,512]{2,3,1,0:T(8,128)(2,1)S(1)} collective-permute-done((bf16[1,1,256,512]{2,3,1,0:T(8,128)(2,1)S(1)}, bf16[1,1,256,512]{2,3,1,0:T(8,128)(2,1)S(1)}, u32[]{:S(2)}, u32[]{:S(2)}) %collective-permute-start.1) | collective-permute-done | bytes 262176 | tf_op jit(solution)/shard_map/ppermute | solution.py:16
  27.8 4.4 %collective-permute-start.2 = (bf16[1,1,256,512]{2,3,1,0:T(8,128)(2,1)S(1)}, bf16[1,1,256,512]{2,3,1,0:T(8,128)(2,1)S(1)}, u32[]{:S(2)}, u32[]{:S(2)}) collective-permute-start(bf16[1,1,256,512]{2,3,1,0:T(8,128)(2,1)S(1)} %collective-permute-done.1), channel_id=1, source_target_pairs={{0,4},{4,8},{8,12},{12,16},{16,20},{20,24},{24,28},{1,5},{5,9},{9,... | collective-permute-start | bytes 786440 | tf_op jit(solution)/shard_map/ppermute | solution.py:16
  32.2 3.9 %collective-permute-done.2 = bf16[1,1,256,512]{2,3,1,0:T(8,128)(2,1)S(1)} collective-permute-done((bf16[1,1,256,512]{2,3,1,0:T(8,128)(2,1)S(1)}, bf16[1,1,256,512]{2,3,1,0:T(8,128)(2,1)S(1)}, u32[]{:S(2)}, u32[]{:S(2)}) %collective-permute-start.2) | collective-permute-done | bytes 262176 | tf_op jit(solution)/shard_map/ppermute | solution.py:16
  36.1 5.3 %collective-permute-start.3 = (bf16[1,1,256,512]{2,3,1,0:T(8,128)(2,1)S(1)}, bf16[1,1,256,512]{2,3,1,0:T(8,128)(2,1)S(1)}, u32[]{:S(2)}, u32[]{:S(2)}) collective-permute-start(bf16[1,1,256,512]{2,3,1,0:T(8,128)(2,1)S(1)} %collective-permute-done.2), channel_id=1, source_target_pairs={{0,4},{4,8},{8,12},{12,16},{16,20},{20,24},{24,28},{1,5},{5,9},{9,... | collective-permute-start | bytes 786440 | tf_op jit(solution)/shard_map/ppermute | solution.py:16
  48.7 80.2 %all-reduce.4.cloned.1.call-done = f32[2,1,256,512]{2,3,1,0:T(8,128)} async-done(((f32[2,1,256,512]{2,3,1,0:T(8,128)}), f32[2,1,256,512]{2,3,1,0:T(8,128)}) %all-reduce.4.cloned.1.call-update) | async-done | bytes 1048592 | tf_op jit(solution)/shard_map/psum | solution.py:83
  129.0 1.9 fusion.18
  132.2 19.8 %all-gather.10.cloned.1.call-done = f32[1,1,512,512]{2,3,1,0:T(8,128)} async-done(((f32[1,1,256,512]{2,3,1,0:T(8,128)}), f32[1,1,512,512]{2,3,1,0:T(8,128)}) %all-gather.10.cloned.1.call-update) | async-done | bytes 1048592 | tf_op jit(solution)/shard_map/all_gather | solution.py:46
  152.0 2.0 fusion.12
  156.2 2.1 fusion.10
  158.3 18.6 %all-gather.16.cloned.1.call-done = f32[512,512]{1,0:T(8,128)} async-done(((f32[256,512]{1,0:T(8,128)}), f32[512,512]{1,0:T(8,128)}) %all-gather.16.cloned.1.call-update) | async-done | bytes 1048592 | tf_op jit(solution)/shard_map/all_gather | solution.py:42
  176.8 3.1 fusion
  180.0 21.4 %all-gather.18.cloned.1.call-done = f32[512,512]{1,0:T(8,128)} async-done(((f32[256,512]{1,0:T(8,128)}), f32[512,512]{1,0:T(8,128)}) %all-gather.18.cloned.1.call-update) | async-done | bytes 1048592 | tf_op jit(solution)/shard_map/all_gather | solution.py:42
  201.4 3.8 %select_bitcast_fusion.1 = (bf16[1,1,256,512]{2,3,1,0:T(8,128)(2,1)}, bf16[1,1,256,512]{2,3,1,0:T(8,128)(2,1)}) fusion(pred[]{:T(512)S(6)} %eq.72, pred[]{:T(512)S(6)} %eq.76, f32[512,512]{1,0:T(8,128)} %all-gather.18.cloned.1.call-done, f32[1,256,512]{2,1,0:T(8,128)S(1)} %copy-done.4), kind=kOutput, calls=%fused_computation.41 | convolution fusion | flops 805699584 | bytes 2097154 | tf_op jit(solution)/shard_map/esij,esjk->esik/dot_general | solution.py:38
  205.3 1.6 collective-permute-start.4
  209.0 69.2 %all-reduce.6.cloned.1.call-done = (bf16[1,1,256,512]{2,3,1,0:T(8,128)(2,1)}, bf16[1,1,256,512]{2,3,1,0:T(8,128)(2,1)}) async-done(((bf16[1,1,256,512]{2,3,1,0:T(8,128)(2,1)}, bf16[1,1,256,512]{2,3,1,0:T(8,128)(2,1)}), (bf16[1,1,256,512]{2,3,1,0:T(8,128)(2,1)}, bf16[1,1,256,512]{2,3,1,0:T(8,128)(2,1)})) %all-reduce.6.cloned.1.call-update) | async-done | bytes 524304 | tf_op jit(solution)/shard_map/psum | solution.py:21
  283.4 17.7 %all-gather.12.cloned.1.call-done = f32[1,1,512,512]{2,3,1,0:T(8,128)} async-done(((f32[1,1,256,512]{2,3,1,0:T(8,128)}), f32[1,1,512,512]{2,3,1,0:T(8,128)}) %all-gather.12.cloned.1.call-update) | async-done | bytes 1048592 | tf_op jit(solution)/shard_map/all_gather | solution.py:46
  301.1 2.3 fusion.8
  303.4 21.1 %all-gather.14.cloned.1.call-done = f32[1,1,512,512]{2,3,1,0:T(8,128)} async-done(((f32[1,1,256,512]{2,3,1,0:T(8,128)}), f32[1,1,512,512]{2,3,1,0:T(8,128)}) %all-gather.14.cloned.1.call-update) | async-done | bytes 1048592 | tf_op jit(solution)/shard_map/all_gather | solution.py:42
  324.6 3.2 fusion.1
  330.4 18.8 %all-gather.20.cloned.1.call-done = f32[512,512]{1,0:T(8,128)} async-done(((f32[256,512]{1,0:T(8,128)}), f32[512,512]{1,0:T(8,128)}) %all-gather.20.cloned.1.call-update) | async-done | bytes 1048592 | tf_op jit(solution)/shard_map/all_gather | solution.py:42
  349.2 3.1 fusion.3
  (62 shorter events, 15.9 us)
Async XLA Ops:
  7.2 121.8 %all-reduce.4.cloned.1.call-start = ((), (), s32[]{:S(2)}) async-start(), calls=%async_computation | async-start | bytes 2097152 | tf_op jit(solution)/shard_map/psum | solution.py:83
  8.3 10.4 %collective-permute-start = (bf16[1,1,256,512]{2,3,1,0:T(8,128)(2,1)S(1)}, bf16[1,1,256,512]{2,3,1,0:T(8,128)(2,1)S(1)}, u32[]{:S(2)}, u32[]{:S(2)}) collective-permute-start(bf16[1,1,256,512]{2,3,1,0:T(8,128)(2,1)S(1)} %copy.17), channel_id=1, source_target_pairs={{0,4},{4,8},{8,12},{12,16},{16,20},{20,24},{24,28},{1,5},{5,9},{9,... | collective-permute-start | bytes 786440 | tf_op jit(solution)/shard_map/ppermute | solution.py:16
  18.7 9.1 %collective-permute-start.1 = (bf16[1,1,256,512]{2,3,1,0:T(8,128)(2,1)S(1)}, bf16[1,1,256,512]{2,3,1,0:T(8,128)(2,1)S(1)}, u32[]{:S(2)}, u32[]{:S(2)}) collective-permute-start(bf16[1,1,256,512]{2,3,1,0:T(8,128)(2,1)S(1)} %collective-permute-done), channel_id=1, source_target_pairs={{0,4},{4,8},{8,12},{12,16},{16,20},{20,24},{24,28},{1,5},{5,9},{9,... | collective-permute-start | bytes 786440 | tf_op jit(solution)/shard_map/ppermute | solution.py:16
  27.8 8.3 %collective-permute-start.2 = (bf16[1,1,256,512]{2,3,1,0:T(8,128)(2,1)S(1)}, bf16[1,1,256,512]{2,3,1,0:T(8,128)(2,1)S(1)}, u32[]{:S(2)}, u32[]{:S(2)}) collective-permute-start(bf16[1,1,256,512]{2,3,1,0:T(8,128)(2,1)S(1)} %collective-permute-done.1), channel_id=1, source_target_pairs={{0,4},{4,8},{8,12},{12,16},{16,20},{20,24},{24,28},{1,5},{5,9},{9,... | collective-permute-start | bytes 786440 | tf_op jit(solution)/shard_map/ppermute | solution.py:16
  36.1 11.1 %collective-permute-start.3 = (bf16[1,1,256,512]{2,3,1,0:T(8,128)(2,1)S(1)}, bf16[1,1,256,512]{2,3,1,0:T(8,128)(2,1)S(1)}, u32[]{:S(2)}, u32[]{:S(2)}) collective-permute-start(bf16[1,1,256,512]{2,3,1,0:T(8,128)(2,1)S(1)} %collective-permute-done.2), channel_id=1, source_target_pairs={{0,4},{4,8},{8,12},{12,16},{16,20},{20,24},{24,28},{1,5},{5,9},{9,... | collective-permute-start | bytes 786440 | tf_op jit(solution)/shard_map/ppermute | solution.py:16
  47.3 1.2 copy-start.4
  48.4 103.6 %all-gather.10.cloned.1.call-start = ((), (), s32[]{:S(2)}) async-start(), calls=%async_computation.1 | async-start | bytes 1572864 | tf_op jit(solution)/shard_map/all_gather | solution.py:46
  48.7 82.3 %copy-start.8 = (s32[2]{0:T(128)S(1)}, s32[2]{0:T(128)}, u32[]{:S(2)}) copy-start(s32[2]{0:T(128)} %param.15) | copy-start | bytes 28
  130.9 45.9 %all-gather.16.cloned.1.call-start = ((), (), s32[]{:S(2)}) async-start(), calls=%async_computation.4 | async-start | bytes 1572864 | tf_op jit(solution)/shard_map/all_gather | solution.py:42
  154.0 2.2 copy-start.3
  155.4 21.5 %copy-start.1 = (f32[256,512]{1,0:T(8,128)S(1)}, f32[256,512]{1,0:T(8,128)}, u32[]{:S(2)}) copy-start(f32[256,512]{1,0:T(8,128)} %fusion.4) | copy-start | bytes 1572868
  155.4 46.0 %all-gather.18.cloned.1.call-start = ((), (), s32[]{:S(2)}) async-start(), calls=%async_computation.5 | async-start | bytes 1572864 | tf_op jit(solution)/shard_map/all_gather | solution.py:42
  179.9 98.3 %all-reduce.6.cloned.1.call-start = ((), (), s32[]{:S(2)}) async-start(), calls=%async_computation.7 | async-start | bytes 1048576 | tf_op jit(solution)/shard_map/psum | solution.py:21
  180.0 28.2 %copy-start.7 = (f32[1,256,512]{2,1,0:T(8,128)S(1)}, f32[1,256,512]{2,1,0:T(8,128)}, u32[]{:S(2)}) copy-start(f32[1,256,512]{2,1,0:T(8,128)} %param.12) | copy-start | bytes 1572868
  205.2 95.9 %all-gather.12.cloned.1.call-start = ((), (), s32[]{:S(2)}) async-start(), calls=%async_computation.2 | async-start | bytes 1572864 | tf_op jit(solution)/shard_map/all_gather | solution.py:46
  205.3 74.2 %collective-permute-start.4 = (bf16[1,1,256,512]{2,3,1,0:T(8,128)(2,1)S(1)}, bf16[1,1,256,512]{2,3,1,0:T(8,128)(2,1)S(1)}, u32[]{:S(2)}, u32[]{:S(2)}) collective-permute-start(bf16[1,1,256,512]{2,3,1,0:T(8,128)(2,1)S(1)} %copy.17), channel_id=1, source_target_pairs={{0,2},{1,3},{4,6},{5,7},{8,10},{9,11},{12,14},{13,15},{16,18},{17,... | collective-permute-start | bytes 786440 | tf_op jit(solution)/shard_map/ppermute | solution.py:31
  206.9 72.6 %collective-permute-start.5 = (bf16[1,1,256,512]{2,3,1,0:T(8,128)(2,1)S(1)}, bf16[1,1,256,512]{2,3,1,0:T(8,128)(2,1)S(1)}, u32[]{:S(2)}, u32[]{:S(2)}) collective-permute-start(bf16[1,1,256,512]{2,3,1,0:T(8,128)(2,1)S(1)} %copy.17), channel_id=1, source_target_pairs={{2,0},{3,1},{6,4},{7,5},{10,8},{11,9},{14,12},{15,13},{18,16},{19,... | collective-permute-start | bytes 786440 | tf_op jit(solution)/shard_map/ppermute | solution.py:32
  280.5 44.1 %all-gather.14.cloned.1.call-start = ((), (), s32[]{:S(2)}) async-start(), calls=%async_computation.3 | async-start | bytes 1572864 | tf_op jit(solution)/shard_map/all_gather | solution.py:42
  281.4 67.8 %all-gather.20.cloned.1.call-start = ((), (), s32[]{:S(2)}) async-start(), calls=%async_computation.6 | async-start | bytes 1572864 | tf_op jit(solution)/shard_map/all_gather | solution.py:42
  324.6 3.2 copy-start.5
  324.6 3.2 copy-start.6
  327.7 1.1 copy-start
  327.7 1.6 copy-start.2
Sparse Core Ops, SparseCore 0:
  48.5 80.3 all-reduce.3
  131.1 20.8 all-gather.9
  155.5 21.2 all-gather.15
  180.1 21.2 all-gather.17
  205.3 72.8 all-reduce.5
  280.6 20.4 all-gather.11
  303.2 21.2 all-gather.13
  327.9 21.2 all-gather.19
where the time goes:
time: 360 us; the launch traced here: 359 us
  waiting for transfers between devices  281 us (78%)
  starting transfers between devices  22.3 us (6%)
  matrix products  21.9 us (6%)
  between operations  20.4 us (6%)
  other arithmetic  8.24 us (2%)
  local copies, waits for them, and re-layouts  5.22 us (1%)
    psum x1, waiting for transfers between devices, body(): polarization = lax.psum(partial_value, 'energy')  80.2 us
    all_gather x4, waiting for transfers between devices, full_rows(): return lax.all_gather(block_rows, 'rep', axis=2, tiled=True)  79.9 us
    psum x1, waiting for transfers between devices, broadcast(): return lax.psum(block, axis)  69.2 us
    all_gather x2, waiting for transfers between devices, newton_rows(): operator_full = lax.all_gather(operator, 'rep', axis=2, tiled=True)  37.5 us
    dot_general x9, matrix products, row_product(): jnp.einsum('esij,esjk->esik', first_factor, second_factor, precision=prec...  21.9 us
    ppermute x4, starting transfers between devices, from_behind(): return lax.ppermute(block, axis, route)  18.9 us
    ppermute x4, waiting for transfers between devices, from_behind(): return lax.ppermute(block, axis, route)  14.1 us
  transfers between devices with their start and end apart: 14, of which 11 were waited for; matrix products, arithmetic and copies ran while one was open for 4% of the time, Pallas kernels for 0%

commit v1 on v0

--- a/solution.py
+++ b/solution.py
@@ -18,7 +18,7 @@
 
 def broadcast(block, axis, owner):
     block = jnp.where(lax.axis_index(axis) == owner, block, jnp.zeros_like(block))
-    return lax.psum(block, axis)
+    return jnp.sum(lax.all_gather(block, axis), axis=0)
 
 
 def with_halo(value, sides, width):

time: 360 us -> 390 us (1.083)
  waiting for transfers between devices: 281 us -> 305 us
  local copies, waits for them, and re-layouts: 5.22 us -> 9.77 us
    all_gather x0 -> x2, waiting for transfers between devices: none -> 93.1 us  [broadcast(): return jnp.sum(lax.all_gather(block, axis), axis=0)]
    psum x1 -> x0, waiting for transfers between devices: 69.2 us -> none  [broadcast(): return lax.psum(block, axis)]
    unnamed x26 -> x24, local copies, waits for them, and re-layouts: 3.05 us -> 7.6 us
  transfers between devices with their start and end apart: 14 -> 15, of which waited for: 11 -> 12; matrix products, arithmetic and copies ran while one was open for 4% -> 5% of each run, Pallas kernels for 0% -> 0%
where the time goes in v1:
time: 390 us; the launch traced here: 389 us
  waiting for transfers between devices  305 us (78%)
  starting transfers between devices  22.3 us (6%)
  matrix products  21.8 us (6%)
  between operations  20.1 us (5%)
  other arithmetic  10.2 us (3%)
  local copies, waits for them, and re-layouts  9.77 us (3%)
    all_gather x2, waiting for transfers between devices, broadcast(): return jnp.sum(lax.all_gather(block, axis), axis=0)  93.1 us
    psum x1, waiting for transfers between devices, body(): polarization = lax.psum(partial_value, 'energy')  80.2 us
    all_gather x4, waiting for transfers between devices, full_rows(): return lax.all_gather(block_rows, 'rep', axis=2, tiled=True)  79.9 us
    all_gather x2, waiting for transfers between devices, newton_rows(): operator_full = lax.all_gather(operator, 'rep', axis=2, tiled=True)  36.7 us
    dot_general x9, matrix products, row_product(): jnp.einsum('esij,esjk->esik', first_factor, second_factor, precision=prec...  21.8 us
    ppermute x4, starting transfers between devices, from_behind(): return lax.ppermute(block, axis, route)  18.9 us
    ppermute x4, waiting for transfers between devices, from_behind(): return lax.ppermute(block, axis, route)  14.1 us
  transfers between devices with their start and end apart: 15, of which 12 were waited for; matrix products, arithmetic and copies ran while one was open for 5% of the time, Pallas kernels for 0%

profile of v1, /device:TPU:0, one launch (start us, length us, event | category | flops | bytes accessed | tf_op | source)
XLA Modules:
  0.0 389.0 jit_solution(7796659840526777101)
XLA Ops:
  8.3 4.9 %collective-permute-start = (bf16[1,1,256,512]{2,3,1,0:T(8,128)(2,1)S(1)}, bf16[1,1,256,512]{2,3,1,0:T(8,128)(2,1)S(1)}, u32[]{:S(2)}, u32[]{:S(2)}) collective-permute-start(bf16[1,1,256,512]{2,3,1,0:T(8,128)(2,1)S(1)} %copy.14), channel_id=1, source_target_pairs={{0,4},{4,8},{8,12},{12,16},{16,20},{20,24},{24,28},{1,5},{5,9},{9,... | collective-permute-start | bytes 786440 | tf_op jit(solution)/shard_map/ppermute | solution.py:16
  13.2 5.5 %collective-permute-done = bf16[1,1,256,512]{2,3,1,0:T(8,128)(2,1)S(1)} collective-permute-done((bf16[1,1,256,512]{2,3,1,0:T(8,128)(2,1)S(1)}, bf16[1,1,256,512]{2,3,1,0:T(8,128)(2,1)S(1)}, u32[]{:S(2)}, u32[]{:S(2)}) %collective-permute-start) | collective-permute-done | bytes 262176 | tf_op jit(solution)/shard_map/ppermute | solution.py:16
  18.7 4.4 %collective-permute-start.1 = (bf16[1,1,256,512]{2,3,1,0:T(8,128)(2,1)S(1)}, bf16[1,1,256,512]{2,3,1,0:T(8,128)(2,1)S(1)}, u32[]{:S(2)}, u32[]{:S(2)}) collective-permute-start(bf16[1,1,256,512]{2,3,1,0:T(8,128)(2,1)S(1)} %collective-permute-done), channel_id=1, source_target_pairs={{0,4},{4,8},{8,12},{12,16},{16,20},{20,24},{24,28},{1,5},{5,9},{9,... | collective-permute-start | bytes 786440 | tf_op jit(solution)/shard_map/ppermute | solution.py:16
  23.1 4.7 %collective-permute-done.1 = bf16[1,1,256,512]{2,3,1,0:T(8,128)(2,1)S(1)} collective-permute-done((bf16[1,1,256,512]{2,3,1,0:T(8,128)(2,1)S(1)}, bf16[1,1,256,512]{2,3,1,0:T(8,128)(2,1)S(1)}, u32[]{:S(2)}, u32[]{:S(2)}) %collective-permute-start.1) | collective-permute-done | bytes 262176 | tf_op jit(solution)/shard_map/ppermute | solution.py:16
  27.8 4.4 %collective-permute-start.2 = (bf16[1,1,256,512]{2,3,1,0:T(8,128)(2,1)S(1)}, bf16[1,1,256,512]{2,3,1,0:T(8,128)(2,1)S(1)}, u32[]{:S(2)}, u32[]{:S(2)}) collective-permute-start(bf16[1,1,256,512]{2,3,1,0:T(8,128)(2,1)S(1)} %collective-permute-done.1), channel_id=1, source_target_pairs={{0,4},{4,8},{8,12},{12,16},{16,20},{20,24},{24,28},{1,5},{5,9},{9,... | collective-permute-start | bytes 786440 | tf_op jit(solution)/shard_map/ppermute | solution.py:16
  32.2 3.9 collective-permute-done.2
  36.1 5.3 %collective-permute-start.3 = (bf16[1,1,256,512]{2,3,1,0:T(8,128)(2,1)S(1)}, bf16[1,1,256,512]{2,3,1,0:T(8,128)(2,1)S(1)}, u32[]{:S(2)}, u32[]{:S(2)}) collective-permute-start(bf16[1,1,256,512]{2,3,1,0:T(8,128)(2,1)S(1)} %collective-permute-done.2), channel_id=1, source_target_pairs={{0,4},{4,8},{8,12},{12,16},{16,20},{20,24},{24,28},{1,5},{5,9},{9,... | collective-permute-start | bytes 786440 | tf_op jit(solution)/shard_map/ppermute | solution.py:16
  48.7 80.2 %all-reduce.2.cloned.1.call-done = f32[2,1,256,512]{2,3,1,0:T(8,128)} async-done(((f32[2,1,256,512]{2,3,1,0:T(8,128)}), f32[2,1,256,512]{2,3,1,0:T(8,128)}) %all-reduce.2.cloned.1.call-update) | async-done | bytes 1048592 | tf_op jit(solution)/shard_map/psum | solution.py:83
  132.2 19.8 %all-gather.14.cloned.1.call-done = f32[1,1,512,512]{2,3,1,0:T(8,128)} async-done(((f32[1,1,256,512]{2,3,1,0:T(8,128)}), f32[1,1,512,512]{2,3,1,0:T(8,128)}) %all-gather.14.cloned.1.call-update) | async-done | bytes 1048592 | tf_op jit(solution)/shard_map/all_gather | solution.py:46
  156.1 2.1 fusion.10
  158.2 18.6 %all-gather.20.cloned.1.call-done = f32[512,512]{1,0:T(8,128)} async-done(((f32[256,512]{1,0:T(8,128)}), f32[512,512]{1,0:T(8,128)}) %all-gather.20.cloned.1.call-update) | async-done | bytes 1048592 | tf_op jit(solution)/shard_map/all_gather | solution.py:42
  176.8 3.1 fusion
  180.0 21.4 %all-gather.22.cloned.1.call-done = f32[512,512]{1,0:T(8,128)} async-done(((f32[256,512]{1,0:T(8,128)}), f32[512,512]{1,0:T(8,128)}) %all-gather.22.cloned.1.call-update) | async-done | bytes 1048592 | tf_op jit(solution)/shard_map/all_gather | solution.py:42
  201.4 3.8 select_bitcast_fusion.1
  209.8 45.9 %all-gather.24.cloned.1.call-done = bf16[2048,512]{0,1:T(8,128)(2,1)} async-done(((bf16[256,512]{0,1:T(8,128)(2,1)}), bf16[2048,512]{0,1:T(8,128)(2,1)}) %all-gather.24.cloned.1.call-update) | async-done | bytes 2097168 | tf_op jit(solution)/shard_map/all_gather | solution.py:21
  255.7 2.3 copy.22
  259.5 47.2 %all-gather.26.cloned.1.call-done = bf16[2048,512]{0,1:T(8,128)(2,1)} async-done(((bf16[256,512]{0,1:T(8,128)(2,1)}), bf16[2048,512]{0,1:T(8,128)(2,1)}) %all-gather.26.cloned.1.call-update) | async-done | bytes 2097168 | tf_op jit(solution)/shard_map/all_gather | solution.py:21
  306.7 2.3 copy.23
  314.5 16.9 %all-gather.16.cloned.1.call-done = f32[1,1,512,512]{2,3,1,0:T(8,128)} async-done(((f32[1,1,256,512]{2,3,1,0:T(8,128)}), f32[1,1,512,512]{2,3,1,0:T(8,128)}) %all-gather.16.cloned.1.call-update) | async-done | bytes 1048592 | tf_op jit(solution)/shard_map/all_gather | solution.py:46
  331.4 2.3 fusion.8
  333.7 21.1 %all-gather.18.cloned.1.call-done = f32[1,1,512,512]{2,3,1,0:T(8,128)} async-done(((f32[1,1,256,512]{2,3,1,0:T(8,128)}), f32[1,1,512,512]{2,3,1,0:T(8,128)}) %all-gather.18.cloned.1.call-update) | async-done | bytes 1048592 | tf_op jit(solution)/shard_map/all_gather | solution.py:42
  354.8 3.1 fusion.1
  360.6 18.8 %all-gather.28.cloned.1.call-done = f32[512,512]{1,0:T(8,128)} async-done(((f32[256,512]{1,0:T(8,128)}), f32[512,512]{1,0:T(8,128)}) %all-gather.28.cloned.1.call-update) | async-done | bytes 1048592 | tf_op jit(solution)/shard_map/all_gather | solution.py:42
  379.4 3.1 fusion.3
  (65 shorter events, 23.9 us)
Async XLA Ops:
  7.2 121.8 %all-reduce.2.cloned.1.call-start = ((), (), s32[]{:S(2)}) async-start(), calls=%async_computation | async-start | bytes 2097152 | tf_op jit(solution)/shard_map/psum | solution.py:83
  8.3 10.4 %collective-permute-start = (bf16[1,1,256,512]{2,3,1,0:T(8,128)(2,1)S(1)}, bf16[1,1,256,512]{2,3,1,0:T(8,128)(2,1)S(1)}, u32[]{:S(2)}, u32[]{:S(2)}) collective-permute-start(bf16[1,1,256,512]{2,3,1,0:T(8,128)(2,1)S(1)} %copy.14), channel_id=1, source_target_pairs={{0,4},{4,8},{8,12},{12,16},{16,20},{20,24},{24,28},{1,5},{5,9},{9,... | collective-permute-start | bytes 786440 | tf_op jit(solution)/shard_map/ppermute | solution.py:16
  18.7 9.1 %collective-permute-start.1 = (bf16[1,1,256,512]{2,3,1,0:T(8,128)(2,1)S(1)}, bf16[1,1,256,512]{2,3,1,0:T(8,128)(2,1)S(1)}, u32[]{:S(2)}, u32[]{:S(2)}) collective-permute-start(bf16[1,1,256,512]{2,3,1,0:T(8,128)(2,1)S(1)} %collective-permute-done), channel_id=1, source_target_pairs={{0,4},{4,8},{8,12},{12,16},{16,20},{20,24},{24,28},{1,5},{5,9},{9,... | collective-permute-start | bytes 786440 | tf_op jit(solution)/shard_map/ppermute | solution.py:16
  27.8 8.3 %collective-permute-start.2 = (bf16[1,1,256,512]{2,3,1,0:T(8,128)(2,1)S(1)}, bf16[1,1,256,512]{2,3,1,0:T(8,128)(2,1)S(1)}, u32[]{:S(2)}, u32[]{:S(2)}) collective-permute-start(bf16[1,1,256,512]{2,3,1,0:T(8,128)(2,1)S(1)} %collective-permute-done.1), channel_id=1, source_target_pairs={{0,4},{4,8},{8,12},{12,16},{16,20},{20,24},{24,28},{1,5},{5,9},{9,... | collective-permute-start | bytes 786440 | tf_op jit(solution)/shard_map/ppermute | solution.py:16
  36.1 11.1 %collective-permute-start.3 = (bf16[1,1,256,512]{2,3,1,0:T(8,128)(2,1)S(1)}, bf16[1,1,256,512]{2,3,1,0:T(8,128)(2,1)S(1)}, u32[]{:S(2)}, u32[]{:S(2)}) collective-permute-start(bf16[1,1,256,512]{2,3,1,0:T(8,128)(2,1)S(1)} %collective-permute-done.2), channel_id=1, source_target_pairs={{0,4},{4,8},{8,12},{12,16},{16,20},{20,24},{24,28},{1,5},{5,9},{9,... | collective-permute-start | bytes 786440 | tf_op jit(solution)/shard_map/ppermute | solution.py:16
  47.3 1.2 copy-start.4
  48.4 103.6 %all-gather.14.cloned.1.call-start = ((), (), s32[]{:S(2)}) async-start(), calls=%async_computation.1 | async-start | bytes 1572864 | tf_op jit(solution)/shard_map/all_gather | solution.py:46
  48.7 82.3 %copy-start.6 = (s32[2]{0:T(128)S(1)}, s32[2]{0:T(128)}, u32[]{:S(2)}) copy-start(s32[2]{0:T(128)} %param.15) | copy-start | bytes 28
  130.9 45.9 %all-gather.20.cloned.1.call-start = ((), (), s32[]{:S(2)}) async-start(), calls=%async_computation.4 | async-start | bytes 1572864 | tf_op jit(solution)/shard_map/all_gather | solution.py:42
  154.0 2.2 copy-start.3
  155.4 21.5 %copy-start.1 = (f32[256,512]{1,0:T(8,128)S(1)}, f32[256,512]{1,0:T(8,128)}, u32[]{:S(2)}) copy-start(f32[256,512]{1,0:T(8,128)} %fusion.4) | copy-start | bytes 1572868
  155.4 46.0 %all-gather.22.cloned.1.call-start = ((), (), s32[]{:S(2)}) async-start(), calls=%async_computation.5 | async-start | bytes 1572864 | tf_op jit(solution)/shard_map/all_gather | solution.py:42
  179.9 75.8 %all-gather.24.cloned.1.call-start = ((), (), s32[]{:S(2)}) async-start(), calls=%async_computation.6 | async-start | bytes 2359296 | tf_op jit(solution)/shard_map/all_gather | solution.py:21
  180.0 28.9 %copy-start.5 = (f32[1,256,512]{2,1,0:T(8,128)S(1)}, f32[1,256,512]{2,1,0:T(8,128)}, u32[]{:S(2)}) copy-start(f32[1,256,512]{2,1,0:T(8,128)} %param.12) | copy-start | bytes 1572868
  205.2 101.5 %all-gather.26.cloned.1.call-start = ((), (), s32[]{:S(2)}) async-start(), calls=%async_computation.7 | async-start | bytes 2359296 | tf_op jit(solution)/shard_map/all_gather | solution.py:21
  205.8 125.6 %all-gather.16.cloned.1.call-start = ((), (), s32[]{:S(2)}) async-start(), calls=%async_computation.2 | async-start | bytes 1572864 | tf_op jit(solution)/shard_map/all_gather | solution.py:46
  205.8 104.9 %collective-permute-start.4 = (bf16[1,1,256,512]{2,3,1,0:T(8,128)(2,1)S(1)}, bf16[1,1,256,512]{2,3,1,0:T(8,128)(2,1)S(1)}, u32[]{:S(2)}, u32[]{:S(2)}) collective-permute-start(bf16[1,1,256,512]{2,3,1,0:T(8,128)(2,1)S(1)} %copy.14), channel_id=1, source_target_pairs={{0,2},{1,3},{4,6},{5,7},{8,10},{9,11},{12,14},{13,15},{16,18},{17,... | collective-permute-start | bytes 786440 | tf_op jit(solution)/shard_map/ppermute | solution.py:31
  207.4 103.3 %collective-permute-start.5 = (bf16[1,1,256,512]{2,3,1,0:T(8,128)(2,1)S(1)}, bf16[1,1,256,512]{2,3,1,0:T(8,128)(2,1)S(1)}, u32[]{:S(2)}, u32[]{:S(2)}) collective-permute-start(bf16[1,1,256,512]{2,3,1,0:T(8,128)(2,1)S(1)} %copy.14), channel_id=1, source_target_pairs={{2,0},{3,1},{6,4},{7,5},{10,8},{11,9},{14,12},{15,13},{18,16},{19,... | collective-permute-start | bytes 786440 | tf_op jit(solution)/shard_map/ppermute | solution.py:32
  311.8 43.1 %all-gather.18.cloned.1.call-start = ((), (), s32[]{:S(2)}) async-start(), calls=%async_computation.3 | async-start | bytes 1572864 | tf_op jit(solution)/shard_map/all_gather | solution.py:42
  312.7 66.7 %all-gather.28.cloned.1.call-start = ((), (), s32[]{:S(2)}) async-start(), calls=%async_computation.8 | async-start | bytes 1572864 | tf_op jit(solution)/shard_map/all_gather | solution.py:42
  357.9 1.1 copy-start
  357.9 1.6 copy-start.2
Sparse Core Ops, SparseCore 0:
  48.5 80.3 all-reduce.1
  131.1 20.8 all-gather.13
  155.5 21.2 all-gather.19
  180.0 21.2 all-gather.21
  205.3 50.3 all-gather.23
  258.2 48.5 all-gather.25
  311.9 19.4 all-gather.15
  333.5 21.2 all-gather.17
  358.1 21.2 all-gather.27
